TPU v7x, 512 devices: a whole 4x8x8 slice. The times are simulated.
512 devices in a mesh: section: 2 (over core), blk: 32 (over z, y_lo), head: 8 (over y_hi, x).
Axes of the slice: x: 4, y: 8 (y_hi: 2, y_lo: 4; y = y_hi * 4 + y_lo), z: 8, core: 2. Of those that a mesh axis runs over, the one named last changes fastest.
Arguments:
- queries: bfloat16 [2, 8192, 8192], P('section', ('blk', 'head')), may hold values from -96 to 96
- key_vectors: bfloat16 [2, 8192, 1024], P('section', ('blk', 'head')), may hold values from -6 to 6
- value_vectors: bfloat16 [2, 8192, 1024], P('section', ('blk', 'head')), may hold values from -6 to 6
- residual: bfloat16 [8192, 8192], P('blk', 'head'), may hold values from -128 to 128
- pair_order: int32 [32], replicated, may hold values from 0 to 31, as said below
- probe_gain: float32 [2, 8192], P('section', 'head'), may hold values from 0.1 to 1.9
- probe_weight: float32 [2, 8192], P('section', 'head'), may hold values from -0.0625 to 0.0625
Outputs:
- hidden_out: bfloat16 [2, 8192, 8192], P('section', 'blk', 'head')
- rewards: float32 [2, 8192], P('section', 'blk')
Inputs may be any that keep to these rules, and one draw needn't show every extreme that they name: `pair_order`: each value appears once.
All inputs are finite; a program needn't handle non-finite values.
Results may differ from a plain program's by a relative error of at most 0.004.
Values may be sent and summed in bfloat16 or wider, within the bound.
No kernel may reach another device: no remote copies, remote signals or barrier semaphores. Data moves between devices by JAX's collectives and lax.ppermute only.
A program may use at most 64 MiB of HBM per device.

v0:
```python
import jax
import jax.numpy as jnp
from jax import lax
from jax.sharding import PartitionSpec as P

D = 8192
HEADS = 64
KV_HEADS = 8
HEAD_DIM = 128
neg_start = -1e30


def sent_together(arrays, axis, dim, along):
    widths = [a.shape[along] for a in arrays]
    both = jnp.concatenate(arrays, axis=along)
    result = lax.all_gather(both, axis, axis=dim, tiled=True)
    return tuple(jnp.split(result, [sum(widths[:k]) for k in range(1, len(widths))], axis=along))


def passed_along(value, axis, steps):
    count = lax.axis_size(axis)
    initial, last = (max(0, -steps), min(count, count - steps))
    return lax.ppermute(value, axis, [(source, source + steps) for source in range(initial, last)])


def copy_for_each(x, axis):
    copies = jnp.broadcast_to(x, (lax.axis_size(axis), *x.shape))
    return lax.all_to_all(copies, axis, split_axis=0, concat_axis=0, tiled=True)


def of_everyone(x, axis):
    everything = copy_for_each(x, axis)
    return jnp.sum(everything, axis=0)


def together(arrays, axis):
    ends = [0]
    for a in arrays:
        ends.append(ends[-1] + a.size)
    total = of_everyone(jnp.concatenate([a.ravel() for a in arrays]), axis)
    return tuple((total[b:e].reshape(a.shape) for a, b, e in zip(arrays, ends, ends[1:])))


def block_first(pair_order, first_row, span_rows):
    count = pair_order.shape[0]
    shard = first_row // (2 * span_rows)
    second = first_row % (2 * span_rows) // span_rows
    lower = jnp.sum(jnp.where(jnp.arange(count, dtype=jnp.int32) == shard, pair_order, 0))
    which = jnp.where(second == 0, lower, 2 * count - 1 - lower)
    return which * span_rows


def update(state, q_part, q_places, key_block, value_block, key_places, factor):
    maxima, totals, accum = state
    scores = (
        jnp.einsum("tkgd,skd->tkgs", q_part, key_block, preferred_element_type=jnp.float32) * factor
    )
    seen = (key_places[None, :] <= q_places[:, None])[:, None, None, :]
    scores = jnp.where(seen, scores, -jnp.inf)
    new_max = jnp.maximum(maxima, jnp.max(scores, axis=-1))
    rescale = jnp.exp(maxima - new_max)
    weights = jnp.exp(scores - new_max[..., None])
    totals = totals * rescale + jnp.sum(weights, axis=-1)
    accum = accum * rescale[..., None] + jnp.einsum(
        "tkgs,skd->tkgd",
        weights.astype(jnp.bfloat16),
        value_block,
        preferred_element_type=jnp.float32,
    )
    return (new_max, totals, accum)


def body(queries, key_vectors, value_vectors, residual, pair_order, probe_gain, probe_weight):
    head_count = lax.axis_size("head")
    q_local, k_local, v_local = (
        lax.all_to_all(queries[0], "head", split_axis=1, concat_axis=0, tiled=True),
        lax.all_to_all(key_vectors[0], "head", split_axis=1, concat_axis=0, tiled=True),
        lax.all_to_all(value_vectors[0], "head", split_axis=1, concat_axis=0, tiled=True),
    )
    row_count = q_local.shape[0]
    span_rows = row_count // 2
    kv_local = KV_HEADS // head_count
    group = HEADS // KV_HEADS
    query_heads = q_local.reshape(row_count, kv_local, group, HEAD_DIM)
    blk_count = lax.axis_size("blk")
    blk_index = lax.axis_index("blk")
    lower = jnp.sum(jnp.where(jnp.arange(blk_count, dtype=jnp.int32) == blk_index, pair_order, 0))
    q_firsts = (lower * span_rows, (2 * blk_count - 1 - lower) * span_rows)
    factor = HEAD_DIM ** (-0.5)
    offsets = jnp.arange(span_rows, dtype=jnp.int32)

    def empty_state():
        return (
            jnp.full((span_rows, kv_local, group), neg_start, jnp.float32),
            jnp.zeros((span_rows, kv_local, group), jnp.float32),
            jnp.zeros((span_rows, kv_local, group, HEAD_DIM), jnp.float32),
        )

    initial = (empty_state(), empty_state())
    carry = initial
    key_piece, value_piece = sent_together((k_local, v_local), "blk", 0, 1)
    blocks = key_piece.shape[0] // span_rows
    key_blocks = key_piece.reshape(blocks, span_rows, kv_local, HEAD_DIM)
    value_blocks = value_piece.reshape(blocks, span_rows, kv_local, HEAD_DIM)
    firsts = jnp.arange(blocks, dtype=jnp.int32) * span_rows

    def key_block(state, inputs):
        key_block_now, value_block_now, first_row = inputs
        key_base = block_first(pair_order, first_row, span_rows)
        key_places = key_base + offsets
        results = []
        for which_half in range(2):
            q_part = query_heads[which_half * span_rows : (which_half + 1) * span_rows]
            q_places = q_firsts[which_half] + offsets

            def compute(inner):
                return update(
                    inner, q_part, q_places, key_block_now, value_block_now, key_places, factor
                )

            def keep(inner):
                return inner

            results.append(
                lax.cond(
                    key_base <= q_firsts[which_half] + span_rows - 1,
                    compute,
                    keep,
                    state[which_half],
                )
            )
        return ((results[0], results[1]), None)

    carry, _ = lax.scan(key_block, carry, (key_blocks, value_blocks, firsts))
    pieces = [state[2] / state[1][..., None] for state in carry]
    attended = jnp.concatenate(pieces, axis=0).reshape(row_count, kv_local * group * HEAD_DIM)
    section_index = lax.axis_index("section")
    own_stream = (residual.astype(jnp.float32) + attended).astype(jnp.bfloat16)
    handed = passed_along(own_stream, "section", 1)
    later_stream = (handed.astype(jnp.float32) + attended).astype(jnp.bfloat16)
    stream = jnp.where(section_index == 0, own_stream, later_stream)
    widened = stream.astype(jnp.float32)
    squares = jnp.sum(widened * widened, axis=-1)
    products = jnp.sum(widened * probe_gain[0][None, :] * probe_weight[0][None, :], axis=-1)
    squares, products = together((squares, products), "head")
    reward = products * lax.rsqrt(squares / D + 1e-05)
    return (stream[None], reward[None])


def solution(mesh):
    return jax.shard_map(
        body,
        mesh=mesh,
        in_specs=(
            P("section", ("blk", "head"), None),
            P("section", ("blk", "head"), None),
            P("section", ("blk", "head"), None),
            P("blk", "head"),
            P(),
            P("section", "head"),
            P("section", "head"),
        ),
        out_specs=(P("section", "blk", "head"), P("section", "blk")),
        check_vma=False,
    )
```

profile of v0, /device:TPU:8, one launch (start us, length us, event | category | flops | bytes accessed | tf_op | source)
XLA Modules:
  0.0 690.0 jit_solution(1719765255200378845)
XLA Ops:
  8.7 8.7 %all-to-all-start = ((bf16[32,8,128]{2,0,1:T(8,128)(2,1)}), bf16[32,8,128]{2,0,1:T(8,128)(2,1)S(1)}, u32[]{:S(2)}, u32[]{:S(2)}) async-start(bf16[32,8,128]{2,0,1:T(8,128)(2,1)} %copy.42), calls=%async_computation | async-start | bytes 131072 | tf_op jit(solution)/shard_map/all_to_all | solution.py:77
  18.3 9.3 %all-to-all-done = bf16[32,8,128]{2,0,1:T(8,128)(2,1)S(1)} async-done(((bf16[32,8,128]{2,0,1:T(8,128)(2,1)}), bf16[32,8,128]{2,0,1:T(8,128)(2,1)S(1)}, u32[]{:S(2)}, u32[]{:S(2)}) %all-to-all-start) | async-done | bytes 65568 | tf_op jit(solution)/shard_map/all_to_all | solution.py:77
  27.6 12.7 %all_to_all.60 = bf16[32,8,128]{2,0,1:T(8,128)(2,1)S(1)} all-to-all(bf16[32,8,128]{2,0,1:T(8,128)(2,1)S(1)} %copy.43), channel_id=1, replica_groups=mesh['section'=2,'blk'=32,'head'=8] {'head'}, dimensions={1} | all-to-all | bytes 131072 | tf_op jit(solution)/shard_map/all_to_all | solution.py:78
  40.9 1.3 copy.55
  42.3 1.1 copy.44
  43.4 3.5 all-to-all-start.2
  48.8 18.0 %all-to-all-done.2 = bf16[32,8,1024]{2,0,1:T(8,128)(2,1)S(1)} async-done(((bf16[32,8,1024]{2,0,1:T(8,128)(2,1)}), bf16[32,8,1024]{2,0,1:T(8,128)(2,1)S(1)}, u32[]{:S(2)}, u32[]{:S(2)}) %all-to-all-start.2) | async-done | bytes 524320 | tf_op jit(solution)/shard_map/all_to_all | solution.py:76
  67.0 140.6 %all-gather.2.cloned.1.call-done = bf16[8192,256]{1,0:T(8,128)(2,1)} async-done(((bf16[256,256]{1,0:T(8,128)(2,1)}), bf16[8192,256]{1,0:T(8,128)(2,1)}) %all-gather.2.cloned.1.call-update) | async-done | bytes 4194320 | tf_op jit(solution)/shard_map/all_gather | solution.py:16
  207.6 4.5 fusion.39
  212.2 445.3 %while.25 = (s32[]{:T(128)}, f32[128,1,8]{0,2,1:T(8,128)S(1)}, f32[128,1,8]{0,2,1:T(8,128)S(1)}, f32[128,1,8,128]{3,0,2,1:T(8,128)S(1)}, f32[128,1,8]{0,2,1:T(8,...) while((s32[]{:T(128)}, f32[128,1,8]{0,2,1:T(8,128)S(1)}, ...), condition=%wide.region_11.12_spmd.clone.clone, body=%wide.region_1.11_spmd.clone.clone.sunk | while | flops 136616448 | bytes 6232100 | solution.py:134
  225.1 0.9 conditional.9
  233.0 0.9 conditional.8
  246.9 0.9 conditional.9
  247.8 0.9 conditional.8
  267.7 0.9 conditional.9
  281.6 0.9 conditional.9
  295.5 0.9 conditional.9
  309.4 0.9 conditional.9
  337.1 0.9 conditional.9
  581.1 0.9 conditional.8
  659.2 1.3 collective-permute-start
  660.6 1.5 collective-permute-done
  662.1 1.1 fusion.29
  663.2 19.3 %all_to_all.61 = f32[8,1,512]{2,1,0:T(1,128)S(1)} all-to-all(f32[8,1,512]{2,1,0:T(1,128)S(1)} %broadcast_in_dim.54), channel_id=1, replica_groups=mesh['section'=2,'blk'=32,'head'=8] {'head'}, dimensions={0} | all-to-all | bytes 32768 | tf_op jit(solution)/shard_map/all_to_all | solution.py:28
  (991 shorter events, 243.2 us)
Async XLA Ops:
  8.0 38.9 %copy-start.3 = (s32[32]{0:T(128)S(1)}, s32[32]{0:T(128)}, u32[]{:S(2)}) copy-start(s32[32]{0:T(128)} %param.17) | copy-start | bytes 388
  8.7 18.9 %all-to-all-start = ((bf16[32,8,128]{2,0,1:T(8,128)(2,1)}), bf16[32,8,128]{2,0,1:T(8,128)(2,1)S(1)}, u32[]{:S(2)}, u32[]{:S(2)}) async-start(bf16[32,8,128]{2,0,1:T(8,128)(2,1)} %copy.42), calls=%async_computation | async-start | bytes 131072 | tf_op jit(solution)/shard_map/all_to_all | solution.py:77
  17.3 190.3 %all-gather.2.cloned.1.call-start = ((), (), s32[]{:S(2)}) async-start(), calls=%async_computation.4 | async-start | bytes 4325376 | tf_op jit(solution)/shard_map/all_gather | solution.py:16
  43.4 23.5 %all-to-all-start.2 = ((bf16[32,8,1024]{2,0,1:T(8,128)(2,1)}), bf16[32,8,1024]{2,0,1:T(8,128)(2,1)S(1)}, u32[]{:S(2)}, u32[]{:S(2)}) async-start(bf16[32,8,1024]{2,0,1:T(8,128)(2,1)} %copy.44), calls=%async_computation.2 | async-start | bytes 1048576 | tf_op jit(solution)/shard_map/all_to_all | solution.py:76
  657.9 1.0 copy-start
  657.9 4.1 copy-start.1
  658.0 4.1 copy-start.2
  659.2 2.8 collective-permute-start
Sparse Core Ops, SparseCore 0:
  41.1 166.4 all-gather.1
where the time goes:
time: 698 us; the launch traced here: 690 us
  loops' own time  260 us (37%)
  waiting for transfers between devices  169 us (24%)
  local copies, waits for them, and re-layouts  98.7 us (14%)
  other arithmetic  57.1 us (8%)
  matrix products  43.4 us (6%)
  blocking collectives  32 us (5%)
  between operations  15.5 us (2%)
  starting transfers between devices  13.5 us (2%)
    another operation x1, loops' own time, body(): carry, _ = lax.scan(key_block, carry, (key_blocks, value_blocks, firsts))  255 us
    all_gather x1, waiting for transfers between devices, sent_together(): result = lax.all_gather(both, axis, axis=dim, tiled=True)  141 us
    squeeze x64, local copies, waits for them, and re-layouts, body(): carry, _ = lax.scan(key_block, carry, (key_blocks, value_blocks, firsts))  50.4 us
    reduce_sum x64, other arithmetic, block_first(): jnp.sum(jnp.where(jnp.arange(count, dtype=jnp.int32) == shard, pair_order...  40.4 us
    dynamic_slice x64, local copies, waits for them, and re-layouts, body(): carry, _ = lax.scan(key_block, carry, (key_blocks, value_blocks, firsts))  37.6 us
    dot_general x65, matrix products, update(): jnp.einsum('tkgs,skd->tkgd', weights.astype(jnp.bfloat16), value_block, p...  28 us
    all_to_all x1, blocking collectives, copy_for_each(): return lax.all_to_all(copies, axis, split_axis=0, concat_axis=0, tiled=True)  19.3 us
    all_to_all x1, waiting for transfers between devices, body(): lax.all_to_all(queries[0], 'head', split_axis=1, concat_axis=0, tiled=True)  18 us
  transfers between devices with their start and end apart: 4, of which 4 were waited for; matrix products, arithmetic and copies ran while one was open for 1% of the time, Pallas kernels for 0%

commit v1 on v0

--- a/solution.py
+++ b/solution.py
@@ -74,7 +74,12 @@
     head_count = lax.axis_size("head")
     q_local, k_local, v_local = (
         lax.all_to_all(queries[0], "head", split_axis=1, concat_axis=0, tiled=True),
-        lax.all_to_all(key_vectors[0], "head", split_axis=1, concat_axis=0, tiled=True),
+        jnp.concatenate(
+            lax.all_to_all(
+                jnp.stack(jnp.split(key_vectors[0], lax.axis_size("head"), axis=1)), "head", 0, 0
+            ),
+            axis=0,
+        ),
         lax.all_to_all(value_vectors[0], "head", split_axis=1, concat_axis=0, tiled=True),
     )
     row_count = q_local.shape[0]

time: 698 us -> 707 us (1.013)
  local copies, waits for them, and re-layouts: 98.7 us -> 108 us
    unnamed x13 -> x19, local copies, waits for them, and re-layouts: 3.54 us -> 11.8 us
where the time goes in v1:
time: 707 us; the launch traced here: 699 us
  loops' own time  260 us (37%)
  waiting for transfers between devices  169 us (24%)
  local copies, waits for them, and re-layouts  108 us (15%)
  other arithmetic  57.1 us (8%)
  matrix products  43.3 us (6%)
  blocking collectives  32 us (5%)
  between operations  15.5 us (2%)
  starting transfers between devices  13.5 us (2%)
    another operation x1, loops' own time, body(): carry, _ = lax.scan(key_block, carry, (key_blocks, value_blocks, firsts))  255 us
    all_gather x1, waiting for transfers between devices, sent_together(): result = lax.all_gather(both, axis, axis=dim, tiled=True)  141 us
    squeeze x64, local copies, waits for them, and re-layouts, body(): carry, _ = lax.scan(key_block, carry, (key_blocks, value_blocks, firsts))  50.4 us
    reduce_sum x64, other arithmetic, block_first(): jnp.sum(jnp.where(jnp.arange(count, dtype=jnp.int32) == shard, pair_order...  40.5 us
    dynamic_slice x64, local copies, waits for them, and re-layouts, body(): carry, _ = lax.scan(key_block, carry, (key_blocks, value_blocks, firsts))  37.6 us
    dot_general x65, matrix products, update(): jnp.einsum('tkgs,skd->tkgd', weights.astype(jnp.bfloat16), value_block, p...  28 us
    all_to_all x1, blocking collectives, copy_for_each(): return lax.all_to_all(copies, axis, split_axis=0, concat_axis=0, tiled=True)  19.3 us
    all_to_all x1, waiting for transfers between devices, body(): lax.all_to_all(queries[0], 'head', split_axis=1, concat_axis=0, tiled=True)  18 us
  transfers between devices with their start and end apart: 4, of which 4 were waited for; matrix products, arithmetic and copies ran while one was open for 1% of the time, Pallas kernels for 0%

profile of v1, /device:TPU:8, one launch (start us, length us, event | category | flops | bytes accessed | tf_op | source)
XLA Modules:
  0.0 698.7 jit_solution(5658894409696280835)
XLA Ops:
  7.2 1.3 constant_dynamic-update-slice_fusion.7
  8.5 1.3 constant_dynamic-update-slice_fusion.6
  9.8 1.3 constant_dynamic-update-slice_fusion.5
  11.1 1.3 constant_dynamic-update-slice_fusion.4
  12.4 1.3 constant_dynamic-update-slice_fusion.3
  13.7 1.3 constant_dynamic-update-slice_fusion.2
  15.0 1.3 constant_dynamic-update-slice_fusion.1
  16.3 1.3 constant_dynamic-update-slice_fusion
  17.6 8.7 %all-to-all-start = ((bf16[8,32,128]{2,1,0:T(8,128)(2,1)}), bf16[8,32,128]{2,1,0:T(8,128)(2,1)S(1)}, u32[]{:S(2)}, u32[]{:S(2)}) async-start(bf16[8,32,128]{2,1,0:T(8,128)(2,1)} %constant_dynamic-update-slice_fusion), calls=%async_computation | async-start | bytes 131072 | tf_op jit(solution)/shard_map/all_to_all | solution.py:78
  27.1 9.3 %all-to-all-done = bf16[8,32,128]{2,1,0:T(8,128)(2,1)S(1)} async-done(((bf16[8,32,128]{2,1,0:T(8,128)(2,1)}), bf16[8,32,128]{2,1,0:T(8,128)(2,1)S(1)}, u32[]{:S(2)}, u32[]{:S(2)}) %all-to-all-start) | async-done | bytes 65568 | tf_op jit(solution)/shard_map/all_to_all | solution.py:78
  36.5 12.7 %all_to_all.46 = bf16[32,8,128]{2,0,1:T(8,128)(2,1)S(1)} all-to-all(bf16[32,8,128]{2,0,1:T(8,128)(2,1)S(1)} %copy.38), channel_id=1, replica_groups=mesh['section'=2,'blk'=32,'head'=8] {'head'}, dimensions={1} | all-to-all | bytes 131072 | tf_op jit(solution)/shard_map/all_to_all | solution.py:83
  49.8 1.3 copy.49
  51.2 1.1 copy.39
  52.3 3.5 all-to-all-start.2
  57.7 18.0 %all-to-all-done.2 = bf16[32,8,1024]{2,0,1:T(8,128)(2,1)S(1)} async-done(((bf16[32,8,1024]{2,0,1:T(8,128)(2,1)}), bf16[32,8,1024]{2,0,1:T(8,128)(2,1)S(1)}, u32[]{:S(2)}, u32[]{:S(2)}) %all-to-all-start.2) | async-done | bytes 524320 | tf_op jit(solution)/shard_map/all_to_all | solution.py:76
  75.9 140.6 %all-gather.2.cloned.1.call-done = bf16[8192,256]{1,0:T(8,128)(2,1)} async-done(((bf16[256,256]{1,0:T(8,128)(2,1)}), bf16[8192,256]{1,0:T(8,128)(2,1)}) %all-gather.2.cloned.1.call-update) | async-done | bytes 4194320 | tf_op jit(solution)/shard_map/all_gather | solution.py:16
  216.5 4.5 fusion.39
  221.1 445.1 %while.25 = (s32[]{:T(128)}, f32[128,1,8]{0,2,1:T(8,128)S(1)}, f32[128,1,8]{0,2,1:T(8,128)S(1)}, f32[128,1,8,128]{3,0,2,1:T(8,128)S(1)}, f32[128,1,8]{0,2,1:T(8,...) while((s32[]{:T(128)}, f32[128,1,8]{0,2,1:T(8,128)S(1)}, ...), condition=%wide.region_11.12_spmd.clone.clone, body=%wide.region_1.11_spmd.clone.clone.sunk | while | flops 136616448 | bytes 6232100 | solution.py:139
  256.7 0.9 conditional.8
  478.8 0.9 conditional.8
  667.9 1.3 collective-permute-start
  669.2 1.5 collective-permute-done
  670.7 1.1 fusion.29
  671.9 19.3 %all_to_all.47 = f32[8,1,512]{2,1,0:T(1,128)S(1)} all-to-all(f32[8,1,512]{2,1,0:T(1,128)S(1)} %broadcast_in_dim.54), channel_id=1, replica_groups=mesh['section'=2,'blk'=32,'head'=8] {'head'}, dimensions={0} | all-to-all | bytes 32768 | tf_op jit(solution)/shard_map/all_to_all | solution.py:28
  (997 shorter events, 249.0 us)
Async XLA Ops:
  8.5 47.3 %copy-start.3 = (s32[32]{0:T(128)S(1)}, s32[32]{0:T(128)}, u32[]{:S(2)}) copy-start(s32[32]{0:T(128)} %param.17) | copy-start | bytes 388
  17.6 18.9 %all-to-all-start = ((bf16[8,32,128]{2,1,0:T(8,128)(2,1)}), bf16[8,32,128]{2,1,0:T(8,128)(2,1)S(1)}, u32[]{:S(2)}, u32[]{:S(2)}) async-start(bf16[8,32,128]{2,1,0:T(8,128)(2,1)} %constant_dynamic-update-slice_fusion), calls=%async_computation | async-start | bytes 131072 | tf_op jit(solution)/shard_map/all_to_all | solution.py:78
  26.2 190.3 %all-gather.2.cloned.1.call-start = ((), (), s32[]{:S(2)}) async-start(), calls=%async_computation.4 | async-start | bytes 4325376 | tf_op jit(solution)/shard_map/all_gather | solution.py:16
  52.3 23.5 %all-to-all-start.2 = ((bf16[32,8,1024]{2,0,1:T(8,128)(2,1)}), bf16[32,8,1024]{2,0,1:T(8,128)(2,1)S(1)}, u32[]{:S(2)}, u32[]{:S(2)}) async-start(bf16[32,8,1024]{2,0,1:T(8,128)(2,1)} %copy.39), calls=%async_computation.2 | async-start | bytes 1048576 | tf_op jit(solution)/shard_map/all_to_all | solution.py:76
  666.5 1.0 copy-start
  666.6 4.1 copy-start.1
  666.6 4.1 copy-start.2
  667.9 2.8 collective-permute-start
Sparse Core Ops, SparseCore 0:
  50.0 166.4 all-gather.1
